TPU v7x, 32 devices: a whole 2x2x4 slice. The times are simulated.
32 devices in a mesh: tile: 8 (over z, y), chan: 4 (over x, core).
Axes of the slice: x: 2, y: 2, z: 4, core: 2. Of those that a mesh axis runs over, the one named last changes fastest.
Arguments:
- feat: bfloat16 [128, 64, 256], P('tile', 'chan'), may hold values from -6 to 6
- lift: float32 [64], replicated, may hold values from -3 to 3
- dilation4_weight: bfloat16 [3, 3, 64, 64], replicated, may hold values from -0.25 to 0.25
- dilation8_weight: bfloat16 [3, 3, 64, 64], replicated, may hold values from -0.25 to 0.25
- entry_fraction: bfloat16 [2048, 128], P('tile'), may hold values from 0.019897461 to 0.19921875
- entry_target_tile: int32 [2048, 1], P('tile'), may hold values from 0 to 7; in each aligned block of 256 rows (0 to 255, 256 to 511, ...) at most 64 rows name the same one
- entry_owner_tile: int32 [2048], P('tile'), may hold values from 0 to 31
- entry_local_net: int32 [2048], P('tile'), may hold values from 0 to 63
- pin_demand_weight: float32 [2048], P('tile'), may hold values from 0.2 to 2
- pin_local_net: int32 [2048], P('tile'), may hold values from 0 to 63
- pin_global_cell: int32 [2048], P('tile'), may hold values from 0 to 511
Outputs:
- cell_grad: float32 [512], P('tile')
Inputs may be any that keep to these rules, and one draw needn't show every extreme that they name: `entry_target_tile`: among the entries of one tile index, at most 64 name the same destination, and in some tile index exactly 64 do.
All inputs are finite; a program needn't handle non-finite values.
Results may differ from a plain program's by a relative error of at most 0.0003.
Values may be sent and summed in bfloat16 or wider, within the bound.
A program may use at most 64 MiB of HBM per device.

v0:
```python
import jax
import jax.numpy as jnp
from jax import lax
from jax.sharding import PartitionSpec as P

NET_DEV = 64
CELL_DEV = 64
TILE_DEV = 32


def extended(array, sides, width):
    for axis, dim in sides:
        peers, length = (lax.axis_size(axis), array.shape[dim])
        up = [(i, (i + 1) % peers) for i in range(peers - 1)]
        down = [(j, i) for i, j in up]
        last = lax.slice_in_dim(array, length - width, length, axis=dim)
        leading = lax.slice_in_dim(array, 0, width, axis=dim)
        before = lax.ppermute(last, axis, up)
        after = lax.ppermute(leading, axis, down)
        array = jnp.concatenate([before, array, after], axis=dim)
    return array


def flipped_kernel(kernel):
    return jnp.transpose(kernel[::-1, ::-1], (0, 1, 3, 2))


def dilated_convolution(own_part, weights, channel_start, dilation):
    row_count, chan_own, col_count = own_part.shape
    rimmed = extended(own_part, (("tile", 0),), dilation)
    own_weights = lax.dynamic_slice_in_dim(weights, channel_start, chan_own, 3)
    start_sum = jnp.zeros((row_count, chan_own, col_count), jnp.float32)
    running = start_sum
    widened = jnp.pad(
        lax.all_gather(rimmed, "chan", axis=1, tiled=True), ((0, 0), (0, 0), (dilation, dilation))
    )
    for row_tap in range(3):
        for col_tap in range(3):
            part_in = widened[
                row_tap * dilation : row_tap * dilation + row_count,
                :,
                col_tap * dilation : col_tap * dilation + col_count,
            ]
            running = running + jnp.einsum(
                "rcw,co->row",
                part_in,
                own_weights[row_tap, col_tap],
                preferred_element_type=jnp.float32,
            )
    return running


def local(
    feat,
    lift,
    dilation4_weight,
    dilation8_weight,
    entry_fraction,
    entry_target_tile,
    entry_owner_tile,
    entry_local_net,
    pin_demand_weight,
    pin_local_net,
    pin_global_cell,
):
    highest = lax.Precision.HIGHEST
    tile_count = lax.axis_size("tile")
    chan_count = lax.axis_size("chan")
    row_count, chan_own, col_count = feat.shape
    channel_start = lax.axis_index("chan") * chan_own
    lift_own = lax.dynamic_slice_in_dim(lift, channel_start, chan_own, 0)
    entry_count = entry_target_tile.shape[0]
    capacity = chan_count * max(1, 2 * entry_count // (chan_count * tile_count))
    part_total = 1
    part_id = 0
    slot_count = capacity // part_total
    destination = entry_target_tile[:, 0]
    dest_hot = (destination[:, None] == jnp.arange(tile_count, dtype=jnp.int32)[None, :]).astype(
        jnp.int32
    )
    rank = jnp.sum(jnp.cumsum(dest_hot, axis=0) * dest_hot, axis=1) - 1
    placed = rank % part_total == part_id
    slot_row = jnp.where(
        placed, destination * slot_count + rank // part_total, tile_count * slot_count
    )
    pin_hot = (pin_local_net[None, :] == jnp.arange(NET_DEV, dtype=jnp.int32)[:, None]).astype(
        jnp.float32
    )
    strength = jnp.dot(pin_hot, pin_demand_weight, precision=highest)
    entry_hot = (entry_local_net[:, None] == jnp.arange(NET_DEV, dtype=jnp.int32)[None, :]).astype(
        jnp.float32
    )
    entry_strength = jnp.dot(entry_hot, strength, precision=highest)
    frac = entry_fraction.astype(jnp.float32)
    payload = entry_strength[:, None] * frac
    send_rows = (
        jnp.zeros((tile_count * slot_count, 128), jnp.float32)
        .at[slot_row]
        .set(payload, mode="drop")
    )
    send_ids = (
        jnp.zeros((tile_count * slot_count,), jnp.int32)
        .at[slot_row]
        .set(entry_owner_tile, mode="drop")
    )
    arrived, arrived_ids = (
        lax.all_to_all(
            send_rows.reshape(tile_count, slot_count, 128).astype(jnp.bfloat16),
            "tile",
            split_axis=0,
            concat_axis=0,
            tiled=True,
        ).astype(jnp.float32),
        lax.all_to_all(
            send_ids.reshape(tile_count, slot_count),
            "tile",
            split_axis=0,
            concat_axis=0,
            tiled=True,
        ),
    )
    tile_hot = (
        arrived_ids.reshape(-1)[:, None] == jnp.arange(TILE_DEV, dtype=jnp.int32)[None, :]
    ).astype(jnp.float32)
    tiles = jnp.dot(tile_hot.T, arrived.reshape(-1, 128), precision=highest)
    demand = (
        tiles.reshape(row_count // 8, col_count // 16, 8, 16)
        .transpose(0, 2, 1, 3)
        .reshape(row_count, col_count)
    )
    input_features = (
        feat.astype(jnp.float32) + demand[:, None, :] * lift_own[None, :, None]
    ).astype(jnp.bfloat16)
    first_preactivation = dilated_convolution(input_features, dilation4_weight, channel_start, 4)
    hidden_features = jax.nn.silu(first_preactivation).astype(jnp.bfloat16)
    second_output = dilated_convolution(hidden_features, dilation8_weight, channel_start, 8)
    second_gradient = jax.nn.sigmoid(second_output).astype(jnp.bfloat16)
    hidden_gradient = dilated_convolution(
        second_gradient, flipped_kernel(dilation8_weight), channel_start, 8
    )
    sigmoid_pre = jax.nn.sigmoid(first_preactivation)
    preactivation_gradient = (
        hidden_gradient * sigmoid_pre * (1.0 + first_preactivation * (1.0 - sigmoid_pre))
    ).astype(jnp.bfloat16)
    inputs_gradient = dilated_convolution(
        preactivation_gradient, flipped_kernel(dilation4_weight), channel_start, 4
    )
    partial_grad = jnp.sum(inputs_gradient * lift_own[None, :, None], axis=1)
    grad_demand = lax.psum(partial_grad, "chan")
    grad_tiles = (
        grad_demand.reshape(row_count // 8, 8, col_count // 16, 16)
        .transpose(0, 2, 1, 3)
        .reshape(TILE_DEV, 128)
    )
    slot_grads = jnp.dot(tile_hot, grad_tiles, precision=highest).reshape(
        tile_count, slot_count, 128
    )
    returned = lax.all_to_all(
        slot_grads.astype(jnp.bfloat16), "tile", split_axis=0, concat_axis=0, tiled=True
    ).astype(slot_grads.dtype)
    entry_rows = jnp.take(returned.reshape(-1, 128), slot_row, axis=0, mode="fill", fill_value=0.0)
    entry_grad = jnp.sum(entry_rows * frac, axis=1)
    grad_net = jnp.dot(entry_grad, entry_hot, precision=highest)
    pin_grad = jnp.dot(grad_net, pin_hot, precision=highest)
    cell_term = jax.ops.segment_sum(pin_grad, pin_global_cell, num_segments=CELL_DEV * tile_count)
    return lax.psum_scatter(cell_term, "tile", scatter_dimension=0, tiled=True)


def solution(mesh):
    in_specs = (
        P("tile", "chan", None),
        P(),
        P(),
        P(),
        P("tile", None),
        P("tile", None),
        P("tile"),
        P("tile"),
        P("tile"),
        P("tile"),
        P("tile"),
    )
    out_specs = P("tile")
    return jax.shard_map(local, mesh=mesh, in_specs=in_specs, out_specs=out_specs, check_vma=False)
```

profile of v0, /device:TPU:0, one launch (start us, length us, event | category | flops | bytes accessed | tf_op | source)
XLA Modules:
  0.0 194.8 jit_solution(14243430125302070767)
XLA Ops:
  6.5 0.7 fusion.60
  7.3 0.6 reduce-window.6
  8.1 0.8 fusion.59
  8.9 0.7 and_reduce_fusion
  9.6 1.6 scatter_custom_fusion
  11.1 0.7 all_to_all.12
  11.8 7.3 %all-to-all-start = ((s32[8,1,64]{2,1,0:T(1,128)}), s32[8,1,64]{2,1,0:T(1,128)S(1)}, u32[]{:S(2)}, u32[]{:S(2)}) async-start(s32[8,1,64]{2,1,0:T(1,128)} %all_to_all.12), calls=%async_computation | async-start | bytes 8192 | tf_op jit(solution)/shard_map/all_to_all | solution.py:114
  19.1 0.8 convolution_bitcast_fusion.2
  19.9 0.9 fusion.42
  20.8 1.7 scatter_custom_fusion.1
  22.5 0.7 convert_element_type.46
  23.2 2.4 %all-to-all-done = s32[8,1,64]{2,1,0:T(1,128)S(1)} async-done(((s32[8,1,64]{2,1,0:T(1,128)}), s32[8,1,64]{2,1,0:T(1,128)S(1)}, u32[]{:S(2)}, u32[]{:S(2)}) %all-to-all-start) | async-done | bytes 2080 | tf_op jit(solution)/shard_map/all_to_all | solution.py:114
  25.6 3.6 %all-to-all-start.1 = ((bf16[8,64,128]{2,1,0:T(8,128)(2,1)}), bf16[8,64,128]{2,1,0:T(8,128)(2,1)S(1)}, u32[]{:S(2)}, u32[]{:S(2)}) async-start(bf16[8,64,128]{2,1,0:T(8,128)(2,1)} %bitcast.24), calls=%async_computation.1 | async-start | bytes 262144 | tf_op jit(solution)/shard_map/all_to_all | solution.py:107
  29.3 0.5 broadcast.170
  29.8 0.7 reduce.8
  30.5 5.9 %all-to-all-done.1 = bf16[8,64,128]{2,1,0:T(8,128)(2,1)S(1)} async-done(((bf16[8,64,128]{2,1,0:T(8,128)(2,1)}), bf16[8,64,128]{2,1,0:T(8,128)(2,1)S(1)}, u32[]{:S(2)}, u32[]{:S(2)}) %all-to-all-start.1) | async-done | bytes 131104 | tf_op jit(solution)/shard_map/all_to_all | solution.py:107
  37.2 1.3 collective-permute-start.1
  38.5 4.5 %collective-permute-start = (bf16[4,16,256]{2,1,0:T(8,128)(2,1)S(1)}, bf16[4,16,256]{2,1,0:T(8,128)(2,1)S(1)}, u32[]{:S(2)}, u32[]{:S(2)}) collective-permute-start(bf16[4,16,256]{2,1,0:T(8,128)(2,1)S(1)} %get-tuple-element.13), channel_id=1, source_target_pairs={{0,4},{4,8},{8,12},{12,16},{16,20},{20,24},{24,28},{1,5},{5,9},{9,... | collective-permute-start | bytes 98312 | tf_op jit(solution)/shard_map/ppermute | solution.py:18
  43.1 1.6 collective-permute-done
  44.7 8.6 %all_gather.12 = bf16[24,64,256]{2,1,0:T(8,128)(2,1)S(1)} all-gather(bf16[24,16,256]{2,1,0:T(8,128)(2,1)S(1)} %pad_maximum_fusion.2), channel_id=1, replica_groups=mesh['tile'=8,'chan'=4] {'chan'}, dimensions={1}, use_global_device_ids=true | all-gather | bytes 983040 | tf_op jit(solution)/shard_map/all_gather | solution.py:35
  53.6 0.4 fusion.8
  53.9 0.4 convolution_add_fusion.21
  54.3 0.4 convolution_add_fusion.20
  55.0 0.4 convolution_add_fusion.18
  55.3 0.4 convolution_add_fusion.17
  56.0 0.4 multiply_convert_fusion
  56.4 1.3 collective-permute-start.3
  57.7 4.9 %collective-permute-start.2 = (bf16[8,16,256]{2,1,0:T(8,128)(2,1)S(1)}, bf16[8,16,256]{2,1,0:T(8,128)(2,1)S(1)}, u32[]{:S(2)}, u32[]{:S(2)}) collective-permute-start(bf16[8,16,256]{2,1,0:T(8,128)(2,1)S(1)} %get-tuple-element.11), channel_id=1, source_target_pairs={{0,4},{4,8},{8,12},{12,16},{16,20},{20,24},{24,28},{1,5},{5,9},{9,... | collective-permute-start | bytes 196616 | tf_op jit(solution)/shard_map/ppermute | solution.py:18
  62.6 0.7 collective-permute-done.3
  63.2 1.6 collective-permute-done.2
  64.8 0.8 pad_maximum_fusion
  65.6 17.1 %all-gather.3.cloned.1.call-done = bf16[32,64,256]{2,1,0:T(8,128)(2,1)} async-done(((bf16[32,16,256]{2,1,0:T(8,128)(2,1)}), bf16[32,64,256]{2,1,0:T(8,128)(2,1)}) %all-gather.3.cloned.1.call-update) | async-done | bytes 1048592 | tf_op jit(solution)/shard_map/all_gather | solution.py:35
  82.7 1.5 fusion.33
  84.5 0.4 fusion.32
  84.9 0.4 fusion.31
  85.6 0.4 fusion.30
  85.9 0.4 fusion.29
  86.6 0.4 fusion.28
  86.9 1.6 fusion.46
  88.6 1.3 collective-permute-start.5
  89.9 4.7 %collective-permute-start.4 = (bf16[8,16,256]{2,0,1:T(8,128)(2,1)S(1)}, bf16[8,16,256]{2,0,1:T(8,128)(2,1)S(1)}, u32[]{:S(2)}, u32[]{:S(2)}) collective-permute-start(bf16[8,16,256]{2,0,1:T(8,128)(2,1)S(1)} %get-tuple-element.9), channel_id=1, source_target_pairs={{0,4},{4,8},{8,12},{12,16},{16,20},{20,24},{24,28},{1,5},{5,9},{9,... | collective-permute-start | bytes 196616 | tf_op jit(solution)/shard_map/ppermute | solution.py:18
  94.7 1.6 collective-permute-done.4
  96.3 0.7 pad_maximum_fusion.1
  97.2 18.6 %all-gather.5.cloned.1.call-done = bf16[32,64,256]{2,0,1:T(8,128)(2,1)} async-done(((bf16[32,16,256]{2,0,1:T(8,128)(2,1)}), bf16[32,64,256]{2,0,1:T(8,128)(2,1)}) %all-gather.5.cloned.1.call-update) | async-done | bytes 1048592 | tf_op jit(solution)/shard_map/all_gather | solution.py:35
  115.7 1.8 copy.66
  118.4 0.3 convolution_add_fusion.12
  119.2 0.3 convolution_add_fusion.9
  119.7 0.3 fusion.5
  120.1 1.3 collective-permute-start.7
  121.4 4.5 %collective-permute-start.6 = (bf16[4,16,256]{2,1,0:T(8,128)(2,1)S(1)}, bf16[4,16,256]{2,1,0:T(8,128)(2,1)S(1)}, u32[]{:S(2)}, u32[]{:S(2)}) collective-permute-start(bf16[4,16,256]{2,1,0:T(8,128)(2,1)S(1)} %get-tuple-element.7), channel_id=1, source_target_pairs={{0,4},{4,8},{8,12},{12,16},{16,20},{20,24},{24,28},{1,5},{5,9},{9,... | collective-permute-start | bytes 98312 | tf_op jit(solution)/shard_map/ppermute | solution.py:18
  126.0 1.5 collective-permute-done.6
  127.6 7.5 %all_gather.15 = bf16[24,64,256]{2,1,0:T(8,128)(2,1)S(1)} all-gather(bf16[24,16,256]{2,1,0:T(8,128)(2,1)S(1)} %pad_maximum_fusion.3), channel_id=1, replica_groups=mesh['tile'=8,'chan'=4] {'chan'}, dimensions={1}, use_global_device_ids=true | all-gather | bytes 983040 | tf_op jit(solution)/shard_map/all_gather | solution.py:35
  135.2 0.3 fusion.10
  136.7 0.3 convolution_add_fusion.2
  137.2 0.3 fusion.6
  137.8 11.7 %psum.7 = f32[32,128]{1,0:T(8,128)S(1)} all-reduce(f32[32,128]{1,0:T(8,128)S(1)} %reshape.105), channel_id=1, replica_groups=mesh['tile'=8,'chan'=4] {'chan'}, use_global_device_ids=true, to_apply=%region_6.7 | all-reduce | flops 4096 | bytes 32768 | tf_op jit(solution)/shard_map/psum | solution.py:149
  149.6 1.0 convolution_convert_fusion
  150.6 7.4 %all-to-all-start.2 = ((bf16[8,64,128]{2,1,0:T(8,128)(2,1)}), bf16[8,64,128]{2,1,0:T(8,128)(2,1)S(1)}, u32[]{:S(2)}, u32[]{:S(2)}) async-start(bf16[8,64,128]{2,1,0:T(8,128)(2,1)} %convolution_convert_fusion), calls=%async_computation.2 | async-start | bytes 262144 | tf_op jit(solution)/shard_map/all_to_all | solution.py:158
  158.0 0.6 dynamic-slice.8
  159.3 6.1 %all-to-all-done.2 = bf16[8,64,128]{2,1,0:T(8,128)(2,1)S(1)} async-done(((bf16[8,64,128]{2,1,0:T(8,128)(2,1)}), bf16[8,64,128]{2,1,0:T(8,128)(2,1)S(1)}, u32[]{:S(2)}, u32[]{:S(2)}) %all-to-all-start.2) | async-done | bytes 131104 | tf_op jit(solution)/shard_map/all_to_all | solution.py:158
  165.4 0.7 gather_fusion
  166.7 2.5 %scatter_custom_fusion.2 = f32[512]{0:T(512)S(1)} fusion(s32[256]{0:T(256)} %param.21, f32[256]{0:T(256)S(1)} %bitcast.284, f32[]{:T(128)} %constant.62.clone.1), kind=kCustom, calls=%fused_computation.201 | custom fusion | flops 256 | bytes 2560 | tf_op jit(solution)/shard_map/scatter-add | solution.py:165
  169.2 18.2 %all-reduce.4 = f32[512]{0:T(512)S(1)} all-reduce(f32[512]{0:T(512)S(1)} %scatter_custom_fusion.2), channel_id=2, replica_groups=mesh['tile'=8,'chan'=4] {'tile'}, use_global_device_ids=true, to_apply=%region_9.10.clone | all-reduce | flops 512 | bytes 4096
  187.4 0.6 dynamic-slice.9
  (74 shorter events, 7.3 us)
Async XLA Ops:
  6.5 12.6 %copy-start = (f32[256]{0:T(256)S(1)}, f32[256]{0:T(256)}, u32[]{:S(2)}) copy-start(f32[256]{0:T(256)} %param.19) | copy-start | bytes 3076
  6.5 22.7 %copy-start.8 = (f32[64]{0:T(128)S(1)}, f32[64]{0:T(128)}, u32[]{:S(2)}) copy-start(f32[64]{0:T(128)} %param.12) | copy-start | bytes 772
  6.5 30.5 %copy-start.5 = (bf16[16,16,256]{2,1,0:T(8,128)(2,1)S(1)}, bf16[16,16,256]{2,1,0:T(8,128)(2,1)}, u32[]{:S(2)}) copy-start(bf16[16,16,256]{2,1,0:T(8,128)(2,1)} %param.11) | copy-start | bytes 393220
  11.8 13.8 %all-to-all-start = ((s32[8,1,64]{2,1,0:T(1,128)}), s32[8,1,64]{2,1,0:T(1,128)S(1)}, u32[]{:S(2)}, u32[]{:S(2)}) async-start(s32[8,1,64]{2,1,0:T(1,128)} %all_to_all.12), calls=%async_computation | async-start | bytes 8192 | tf_op jit(solution)/shard_map/all_to_all | solution.py:114
  25.6 10.9 %all-to-all-start.1 = ((bf16[8,64,128]{2,1,0:T(8,128)(2,1)}), bf16[8,64,128]{2,1,0:T(8,128)(2,1)S(1)}, u32[]{:S(2)}, u32[]{:S(2)}) async-start(bf16[8,64,128]{2,1,0:T(8,128)(2,1)} %bitcast.24), calls=%async_computation.1 | async-start | bytes 262144 | tf_op jit(solution)/shard_map/all_to_all | solution.py:107
  29.2 53.6 %all-gather.3.cloned.1.call-start = ((), (), s32[]{:S(2)}) async-start(), calls=%async_computation.3 | async-start | bytes 1310720 | tf_op jit(solution)/shard_map/all_gather | solution.py:35
  36.6 16.7 %copy-start.3 = (bf16[3,3,64,64]{3,2,1,0:T(8,128)(2,1)S(1)}, bf16[3,3,64,64]{3,2,1,0:T(8,128)(2,1)}, u32[]{:S(2)}) copy-start(bf16[3,3,64,64]{3,2,1,0:T(8,128)(2,1)} %param.13) | copy-start | bytes 221188
  37.2 5.9 %collective-permute-start.1 = (bf16[4,16,256]{2,1,0:T(8,128)(2,1)S(1)}, bf16[4,16,256]{2,1,0:T(8,128)(2,1)S(1)}, u32[]{:S(2)}, u32[]{:S(2)}) collective-permute-start(bf16[4,16,256]{2,1,0:T(8,128)(2,1)S(1)} %get-tuple-element.14), channel_id=1, source_target_pairs={{4,0},{8,4},{12,8},{16,12},{20,16},{24,20},{28,24},{5,1},{9,5},{13... | collective-permute-start | bytes 98312 | tf_op jit(solution)/shard_map/ppermute | solution.py:19
  38.5 6.1 %collective-permute-start = (bf16[4,16,256]{2,1,0:T(8,128)(2,1)S(1)}, bf16[4,16,256]{2,1,0:T(8,128)(2,1)S(1)}, u32[]{:S(2)}, u32[]{:S(2)}) collective-permute-start(bf16[4,16,256]{2,1,0:T(8,128)(2,1)S(1)} %get-tuple-element.13), channel_id=1, source_target_pairs={{0,4},{4,8},{8,12},{12,16},{16,20},{20,24},{24,28},{1,5},{5,9},{9,... | collective-permute-start | bytes 98312 | tf_op jit(solution)/shard_map/ppermute | solution.py:18
  56.0 26.7 %copy-start.2 = (bf16[3,3,64,64]{3,2,1,0:T(8,128)(2,1)S(1)}, bf16[3,3,64,64]{3,2,1,0:T(8,128)(2,1)}, u32[]{:S(2)}) copy-start(bf16[3,3,64,64]{3,2,1,0:T(8,128)(2,1)} %param.14) | copy-start | bytes 221188
  56.4 6.8 %collective-permute-start.3 = (bf16[8,16,256]{2,1,0:T(8,128)(2,1)S(1)}, bf16[8,16,256]{2,1,0:T(8,128)(2,1)S(1)}, u32[]{:S(2)}, u32[]{:S(2)}) collective-permute-start(bf16[8,16,256]{2,1,0:T(8,128)(2,1)S(1)} %get-tuple-element.12), channel_id=1, source_target_pairs={{4,0},{8,4},{12,8},{16,12},{20,16},{24,20},{28,24},{5,1},{9,5},{13... | collective-permute-start | bytes 196616 | tf_op jit(solution)/shard_map/ppermute | solution.py:19
  57.7 7.1 %collective-permute-start.2 = (bf16[8,16,256]{2,1,0:T(8,128)(2,1)S(1)}, bf16[8,16,256]{2,1,0:T(8,128)(2,1)S(1)}, u32[]{:S(2)}, u32[]{:S(2)}) collective-permute-start(bf16[8,16,256]{2,1,0:T(8,128)(2,1)S(1)} %get-tuple-element.11), channel_id=1, source_target_pairs={{0,4},{4,8},{8,12},{12,16},{16,20},{20,24},{24,28},{1,5},{5,9},{9,... | collective-permute-start | bytes 196616 | tf_op jit(solution)/shard_map/ppermute | solution.py:18
  65.6 50.2 %all-gather.5.cloned.1.call-start = ((), (), s32[]{:S(2)}) async-start(), calls=%async_computation.4 | async-start | bytes 1310720 | tf_op jit(solution)/shard_map/all_gather | solution.py:35
  82.7 1.5 copy-start.1
  88.6 6.2 %collective-permute-start.5 = (bf16[8,16,256]{2,0,1:T(8,128)(2,1)S(1)}, bf16[8,16,256]{2,0,1:T(8,128)(2,1)S(1)}, u32[]{:S(2)}, u32[]{:S(2)}) collective-permute-start(bf16[8,16,256]{2,0,1:T(8,128)(2,1)S(1)} %get-tuple-element.10), channel_id=1, source_target_pairs={{4,0},{8,4},{12,8},{16,12},{20,16},{24,20},{28,24},{5,1},{9,5},{13... | collective-permute-start | bytes 196616 | tf_op jit(solution)/shard_map/ppermute | solution.py:19
  89.9 6.4 %collective-permute-start.4 = (bf16[8,16,256]{2,0,1:T(8,128)(2,1)S(1)}, bf16[8,16,256]{2,0,1:T(8,128)(2,1)S(1)}, u32[]{:S(2)}, u32[]{:S(2)}) collective-permute-start(bf16[8,16,256]{2,0,1:T(8,128)(2,1)S(1)} %get-tuple-element.9), channel_id=1, source_target_pairs={{0,4},{4,8},{8,12},{12,16},{16,20},{20,24},{24,28},{1,5},{5,9},{9,... | collective-permute-start | bytes 196616 | tf_op jit(solution)/shard_map/ppermute | solution.py:18
  120.1 5.9 %collective-permute-start.7 = (bf16[4,16,256]{2,1,0:T(8,128)(2,1)S(1)}, bf16[4,16,256]{2,1,0:T(8,128)(2,1)S(1)}, u32[]{:S(2)}, u32[]{:S(2)}) collective-permute-start(bf16[4,16,256]{2,1,0:T(8,128)(2,1)S(1)} %get-tuple-element.8), channel_id=1, source_target_pairs={{4,0},{8,4},{12,8},{16,12},{20,16},{24,20},{28,24},{5,1},{9,5},{13... | collective-permute-start | bytes 98312 | tf_op jit(solution)/shard_map/ppermute | solution.py:19
  121.4 6.1 %collective-permute-start.6 = (bf16[4,16,256]{2,1,0:T(8,128)(2,1)S(1)}, bf16[4,16,256]{2,1,0:T(8,128)(2,1)S(1)}, u32[]{:S(2)}, u32[]{:S(2)}) collective-permute-start(bf16[4,16,256]{2,1,0:T(8,128)(2,1)S(1)} %get-tuple-element.7), channel_id=1, source_target_pairs={{0,4},{4,8},{8,12},{12,16},{16,20},{20,24},{24,28},{1,5},{5,9},{9,... | collective-permute-start | bytes 98312 | tf_op jit(solution)/shard_map/ppermute | solution.py:18
  137.2 20.8 %copy-start.9 = (u32[32]{0:T(128)S(1)}, u32[32]{0:T(128)}, u32[]{:S(2)}) copy-start(u32[32]{0:T(128)} %constant.82) | copy-start | bytes 388
  137.8 28.3 %copy-start.4 = (bf16[256,128]{1,0:T(8,128)(2,1)S(1)}, bf16[256,128]{1,0:T(8,128)(2,1)}, u32[]{:S(2)}) copy-start(bf16[256,128]{1,0:T(8,128)(2,1)} %param.15) | copy-start | bytes 196612
  150.6 15.7 %copy-start.6 = (s32[256]{0:T(256)S(1)}, s32[256]{0:T(256)}, u32[]{:S(2)}) copy-start(s32[256]{0:T(256)} %param.18) | copy-start | bytes 3076
  150.6 15.9 %copy-start.7 = (s32[256]{0:T(256)S(1)}, s32[256]{0:T(256)}, u32[]{:S(2)}) copy-start(s32[256]{0:T(256)} %param.20) | copy-start | bytes 3076
  150.6 14.7 %all-to-all-start.2 = ((bf16[8,64,128]{2,1,0:T(8,128)(2,1)}), bf16[8,64,128]{2,1,0:T(8,128)(2,1)S(1)}, u32[]{:S(2)}, u32[]{:S(2)}) async-start(bf16[8,64,128]{2,1,0:T(8,128)(2,1)} %convolution_convert_fusion), calls=%async_computation.2 | async-start | bytes 262144 | tf_op jit(solution)/shard_map/all_to_all | solution.py:158
Sparse Core Ops, SparseCore 0:
  65.7 16.9 all-gather.2
  97.2 18.4 all-gather.4
where the time goes:
time: 196 us; the launch traced here: 195 us
  waiting for transfers between devices  57.2 us (29%)
  blocking collectives  46 us (23%)
  starting transfers between devices  42.2 us (22%)
  matrix products  15.8 us (8%)
  between operations  14.4 us (7%)
  other arithmetic  11.8 us (6%)
  local copies, waits for them, and re-layouts  7.41 us (4%)
    all_gather x2, waiting for transfers between devices, dilated_convolution(): lax.all_gather(rimmed, 'chan', axis=1, tiled=True)  35.7 us
    ppermute x4, starting transfers between devices, extended(): before = lax.ppermute(last, axis, up)  18.7 us
    unnamed x1, blocking collectives  18.2 us
    all_gather x2, blocking collectives, dilated_convolution(): lax.all_gather(rimmed, 'chan', axis=1, tiled=True)  16.1 us
    dot_general x36, matrix products, dilated_convolution(): jnp.einsum('rcw,co->row', part_in, own_weights[row_tap, col_tap], preferr...  12.4 us
    psum x1, blocking collectives, local(): grad_demand = lax.psum(partial_grad, 'chan')  11.7 us
    all_to_all x1, starting transfers between devices, local(): lax.all_to_all(slot_grads.astype(jnp.bfloat16), 'tile', split_axis=0, con...  7.38 us
    all_to_all x1, starting transfers between devices, local(): lax.all_to_all(send_ids.reshape(tile_count, slot_count), 'tile', split_ax...  7.31 us
  transfers between devices with their start and end apart: 13, of which 11 were waited for; matrix products, arithmetic and copies ran while one was open for 3% of the time, Pallas kernels for 0%

commit v1 on v0

--- a/solution.py
+++ b/solution.py
@@ -6,6 +6,11 @@
 NET_DEV = 64
 CELL_DEV = 64
 TILE_DEV = 32
+
+
+def gather_blocks(x, mesh_axis, dim):
+    blocks = lax.all_gather(x, mesh_axis)
+    return jnp.concatenate(blocks, axis=dim)
 
 
 def extended(array, sides, width):
@@ -31,9 +36,7 @@
     own_weights = lax.dynamic_slice_in_dim(weights, channel_start, chan_own, 3)
     start_sum = jnp.zeros((row_count, chan_own, col_count), jnp.float32)
     running = start_sum
-    widened = jnp.pad(
-        lax.all_gather(rimmed, "chan", axis=1, tiled=True), ((0, 0), (0, 0), (dilation, dilation))
-    )
+    widened = jnp.pad(gather_blocks(rimmed, "chan", 1), ((0, 0), (0, 0), (dilation, dilation)))
     for row_tap in range(3):
         for col_tap in range(3):
             part_in = widened[

time: 196 us -> 198 us (1.010)
  starting transfers between devices: 42.2 us -> 34.7 us
  waiting for transfers between devices: 57.2 us -> 64.2 us
  local copies, waits for them, and re-layouts: 7.41 us -> 11.5 us
    ppermute x4, waiting for transfers between devices: 0.79 us -> 17 us  [extended(): after = lax.ppermute(leading, axis, down)]
    ppermute x4, starting transfers between devices: 18.7 us -> 12.8 us  [extended(): before = lax.ppermute(last, axis, up)]
    ppermute x4, waiting for transfers between devices: 6.25 us -> 1.52 us  [extended(): before = lax.ppermute(last, axis, up)]
    all_gather x2, waiting for transfers between devices: 35.7 us -> 31.1 us  [gather_blocks(): blocks = lax.all_gather(x, mesh_axis)]
    slice x1 -> x8, local copies, waits for them, and re-layouts: 0.21 us -> 3.22 us  [the longest x7 3 us: dilated_convolution(): widened[row_tap * dilation:row_tap * dilation + row_count, :, col_tap * d...]
  transfers between devices with their start and end apart: 13 -> 13, of which waited for: 11 -> 13; matrix products, arithmetic and copies ran while one was open for 3% -> 3% of each run, Pallas kernels for 0% -> 0%
where the time goes in v1:
time: 198 us; the launch traced here: 197 us
  waiting for transfers between devices  64.2 us (32%)
  blocking collectives  46 us (23%)
  starting transfers between devices  34.7 us (18%)
  matrix products  14.7 us (7%)
  between operations  14.5 us (7%)
  other arithmetic  11.7 us (6%)
  local copies, waits for them, and re-layouts  11.5 us (6%)
    all_gather x2, waiting for transfers between devices, gather_blocks(): blocks = lax.all_gather(x, mesh_axis)  31.1 us
    unnamed x1, blocking collectives  18.2 us
    ppermute x4, waiting for transfers between devices, extended(): after = lax.ppermute(leading, axis, down)  17 us
    all_gather x2, blocking collectives, gather_blocks(): blocks = lax.all_gather(x, mesh_axis)  16.3 us
    ppermute x4, starting transfers between devices, extended(): before = lax.ppermute(last, axis, up)  12.8 us
    psum x1, blocking collectives, local(): grad_demand = lax.psum(partial_grad, 'chan')  11.5 us
    dot_general x36, matrix products, dilated_convolution(): jnp.einsum('rcw,co->row', part_in, own_weights[row_tap, col_tap], preferr...  11.2 us
    all_to_all x1, starting transfers between devices, local(): lax.all_to_all(send_ids.reshape(tile_count, slot_count), 'tile', split_ax...  7.31 us
  transfers between devices with their start and end apart: 13, of which 13 were waited for; matrix products, arithmetic and copies ran while one was open for 3% of the time, Pallas kernels for 0%

profile of v1, /device:TPU:0, one launch (start us, length us, event | category | flops | bytes accessed | tf_op | source)
XLA Modules:
  0.0 197.3 jit_solution(3670143812291627563)
XLA Ops:
  6.5 0.7 fusion.44
  7.3 0.6 reduce-window.6
  8.1 0.8 fusion.43
  8.9 0.7 and_reduce_fusion
  9.6 1.6 scatter_custom_fusion
  11.1 0.7 all_to_all.12
  11.8 7.3 %all-to-all-start = ((s32[8,1,64]{2,1,0:T(1,128)}), s32[8,1,64]{2,1,0:T(1,128)S(1)}, u32[]{:S(2)}, u32[]{:S(2)}) async-start(s32[8,1,64]{2,1,0:T(1,128)} %all_to_all.12), calls=%async_computation | async-start | bytes 8192 | tf_op jit(solution)/shard_map/all_to_all | solution.py:117
  19.1 0.8 convolution_bitcast_fusion.2
  19.9 0.9 fusion.23
  20.8 1.7 scatter_custom_fusion.1
  22.5 0.7 convert_element_type.46
  23.2 2.4 %all-to-all-done = s32[8,1,64]{2,1,0:T(1,128)S(1)} async-done(((s32[8,1,64]{2,1,0:T(1,128)}), s32[8,1,64]{2,1,0:T(1,128)S(1)}, u32[]{:S(2)}, u32[]{:S(2)}) %all-to-all-start) | async-done | bytes 2080 | tf_op jit(solution)/shard_map/all_to_all | solution.py:117
  25.6 3.6 %all-to-all-start.1 = ((bf16[8,64,128]{2,1,0:T(8,128)(2,1)}), bf16[8,64,128]{2,1,0:T(8,128)(2,1)S(1)}, u32[]{:S(2)}, u32[]{:S(2)}) async-start(bf16[8,64,128]{2,1,0:T(8,128)(2,1)} %bitcast.24), calls=%async_computation.1 | async-start | bytes 262144 | tf_op jit(solution)/shard_map/all_to_all | solution.py:110
  29.3 0.5 broadcast.170
  29.8 0.7 reduce.8
  30.6 5.9 %all-to-all-done.1 = bf16[8,64,128]{2,1,0:T(8,128)(2,1)S(1)} async-done(((bf16[8,64,128]{2,1,0:T(8,128)(2,1)}), bf16[8,64,128]{2,1,0:T(8,128)(2,1)S(1)}, u32[]{:S(2)}, u32[]{:S(2)}) %all-to-all-start.1) | async-done | bytes 131104 | tf_op jit(solution)/shard_map/all_to_all | solution.py:110
  37.2 2.1 %collective-permute-start = (bf16[4,16,256]{2,1,0:T(8,128)(2,1)S(1)}, bf16[4,16,256]{2,1,0:T(8,128)(2,1)S(1)}, u32[]{:S(2)}, u32[]{:S(2)}) collective-permute-start(bf16[4,16,256]{2,1,0:T(8,128)(2,1)S(1)} %get-tuple-element.31), channel_id=1, source_target_pairs={{0,4},{4,8},{8,12},{12,16},{16,20},{20,24},{24,28},{1,5},{5,9},{9,... | collective-permute-start | bytes 98312 | tf_op jit(solution)/shard_map/ppermute | solution.py:23
  39.3 1.3 collective-permute-start.1
  40.9 4.2 %collective-permute-done.1 = bf16[4,16,256]{2,1,0:T(8,128)(2,1)S(1)} collective-permute-done((bf16[4,16,256]{2,1,0:T(8,128)(2,1)S(1)}, bf16[4,16,256]{2,1,0:T(8,128)(2,1)S(1)}, u32[]{:S(2)}, u32[]{:S(2)}) %collective-permute-start.1) | collective-permute-done | bytes 32800 | tf_op jit(solution)/shard_map/ppermute | solution.py:24
  45.2 8.6 %all-gather = bf16[96,16,256]{2,1,0:T(8,128)(2,1)S(1)} all-gather(bf16[24,16,256]{2,1,0:T(8,128)(2,1)S(1)} %pad_maximum_fusion.2), channel_id=2, replica_groups=mesh['tile'=8,'chan'=4] {'chan'}, dimensions={0}, use_global_device_ids=true | all-gather | bytes 983040 | tf_op jit(solution)/shard_map/all_gather | solution.py:12
  54.0 0.7 copy-done.3
  54.8 0.3 fusion.7
  55.4 0.4 convolution_add_fusion.22
  55.8 0.4 convolution_add_fusion.21
  56.4 0.4 convolution_add_fusion.19
  56.8 0.4 convolution_add_fusion.18
  57.5 0.4 multiply_convert_fusion
  57.9 3.9 %collective-permute-start.2 = (bf16[8,16,256]{2,1,0:T(8,128)(2,1)S(1)}, bf16[8,16,256]{2,1,0:T(8,128)(2,1)S(1)}, u32[]{:S(2)}, u32[]{:S(2)}) collective-permute-start(bf16[8,16,256]{2,1,0:T(8,128)(2,1)S(1)} %get-tuple-element.29), channel_id=1, source_target_pairs={{0,4},{4,8},{8,12},{12,16},{16,20},{20,24},{24,28},{1,5},{5,9},{9,... | collective-permute-start | bytes 196616 | tf_op jit(solution)/shard_map/ppermute | solution.py:23
  61.8 1.3 collective-permute-start.3
  63.1 0.6 collective-permute-done.2
  63.7 4.3 %collective-permute-done.3 = bf16[8,16,256]{2,1,0:T(8,128)(2,1)S(1)} collective-permute-done((bf16[8,16,256]{2,1,0:T(8,128)(2,1)S(1)}, bf16[8,16,256]{2,1,0:T(8,128)(2,1)S(1)}, u32[]{:S(2)}, u32[]{:S(2)}) %collective-permute-start.3) | collective-permute-done | bytes 65568 | tf_op jit(solution)/shard_map/ppermute | solution.py:24
  68.0 0.7 pad_maximum_fusion
  68.8 14.4 %all-gather.7.cloned.1.call-done = bf16[128,16,256]{2,1,0:T(8,128)(2,1)} async-done(((bf16[32,16,256]{2,1,0:T(8,128)(2,1)}), bf16[128,16,256]{2,1,0:T(8,128)(2,1)}) %all-gather.7.cloned.1.call-update) | async-done | bytes 1048592 | tf_op jit(solution)/shard_map/all_gather | solution.py:12
  83.1 1.4 copy.178
  84.5 0.4 fusion.12
  84.9 0.4 fusion.10
  85.2 0.4 fusion.11
  85.6 0.4 fusion.13
  85.9 0.4 fusion.9
  86.3 0.4 fusion.14
  87.8 1.6 fusion.27
  89.4 3.4 %collective-permute-start.4 = (bf16[8,16,256]{2,0,1:T(8,128)(2,1)S(1)}, bf16[8,16,256]{2,0,1:T(8,128)(2,1)S(1)}, u32[]{:S(2)}, u32[]{:S(2)}) collective-permute-start(bf16[8,16,256]{2,0,1:T(8,128)(2,1)S(1)} %get-tuple-element.27), channel_id=1, source_target_pairs={{0,4},{4,8},{8,12},{12,16},{16,20},{20,24},{24,28},{1,5},{5,9},{9,... | collective-permute-start | bytes 196616 | tf_op jit(solution)/shard_map/ppermute | solution.py:23
  92.8 1.5 collective-permute-start.5
  94.3 0.4 collective-permute-done.4
  94.7 4.3 %collective-permute-done.5 = bf16[8,16,256]{2,0,1:T(8,128)(2,1)S(1)} collective-permute-done((bf16[8,16,256]{2,0,1:T(8,128)(2,1)S(1)}, bf16[8,16,256]{2,0,1:T(8,128)(2,1)S(1)}, u32[]{:S(2)}, u32[]{:S(2)}) %collective-permute-start.5) | collective-permute-done | bytes 65568 | tf_op jit(solution)/shard_map/ppermute | solution.py:24
  99.0 0.7 pad_maximum_fusion.1
  99.8 16.8 %all-gather.9.cloned.1.call-done = bf16[128,16,256]{2,0,1:T(8,128)(2,1)} async-done(((bf16[32,16,256]{2,0,1:T(8,128)(2,1)}), bf16[128,16,256]{2,0,1:T(8,128)(2,1)}) %all-gather.9.cloned.1.call-update) | async-done | bytes 1048592 | tf_op jit(solution)/shard_map/all_gather | solution.py:12
  116.6 1.6 fusion.91
  118.3 0.6 copy.76
  122.0 0.3 fusion.5
  122.3 3.4 %collective-permute-start.6 = (bf16[4,16,256]{2,1,0:T(8,128)(2,1)S(1)}, bf16[4,16,256]{2,1,0:T(8,128)(2,1)S(1)}, u32[]{:S(2)}, u32[]{:S(2)}) collective-permute-start(bf16[4,16,256]{2,1,0:T(8,128)(2,1)S(1)} %get-tuple-element.25), channel_id=1, source_target_pairs={{0,4},{4,8},{8,12},{12,16},{16,20},{20,24},{24,28},{1,5},{5,9},{9,... | collective-permute-start | bytes 98312 | tf_op jit(solution)/shard_map/ppermute | solution.py:23
  125.7 1.3 collective-permute-start.7
  127.3 4.2 %collective-permute-done.7 = bf16[4,16,256]{2,1,0:T(8,128)(2,1)S(1)} collective-permute-done((bf16[4,16,256]{2,1,0:T(8,128)(2,1)S(1)}, bf16[4,16,256]{2,1,0:T(8,128)(2,1)S(1)}, u32[]{:S(2)}, u32[]{:S(2)}) %collective-permute-start.7) | collective-permute-done | bytes 32800 | tf_op jit(solution)/shard_map/ppermute | solution.py:24
  131.6 7.7 %all-gather.3 = bf16[96,16,256]{2,1,0:T(8,128)(2,1)S(1)} all-gather(bf16[24,16,256]{2,1,0:T(8,128)(2,1)S(1)} %pad_maximum_fusion.3), channel_id=5, replica_groups=mesh['tile'=8,'chan'=4] {'chan'}, dimensions={0}, use_global_device_ids=true | all-gather | bytes 983040 | tf_op jit(solution)/shard_map/all_gather | solution.py:12
  141.7 0.3 fusion.6
  142.3 11.5 %psum.7 = f32[32,128]{1,0:T(8,128)S(1)} all-reduce(f32[32,128]{1,0:T(8,128)S(1)} %reshape.149), channel_id=1, replica_groups=mesh['tile'=8,'chan'=4] {'chan'}, use_global_device_ids=true, to_apply=%region_6.7 | all-reduce | flops 4096 | bytes 32768 | tf_op jit(solution)/shard_map/psum | solution.py:152
  153.9 1.1 convolution_convert_fusion
  154.9 5.6 %all-to-all-start.2 = ((bf16[8,64,128]{2,1,0:T(8,128)(2,1)}), bf16[8,64,128]{2,1,0:T(8,128)(2,1)S(1)}, u32[]{:S(2)}, u32[]{:S(2)}) async-start(bf16[8,64,128]{2,1,0:T(8,128)(2,1)} %convolution_convert_fusion), calls=%async_computation.2 | async-start | bytes 262144 | tf_op jit(solution)/shard_map/all_to_all | solution.py:161
  160.6 0.6 dynamic-slice.8
  161.8 6.1 %all-to-all-done.2 = bf16[8,64,128]{2,1,0:T(8,128)(2,1)S(1)} async-done(((bf16[8,64,128]{2,1,0:T(8,128)(2,1)}), bf16[8,64,128]{2,1,0:T(8,128)(2,1)S(1)}, u32[]{:S(2)}, u32[]{:S(2)}) %all-to-all-start.2) | async-done | bytes 131104 | tf_op jit(solution)/shard_map/all_to_all | solution.py:161
  167.9 0.7 gather_fusion
  169.2 2.5 %scatter_custom_fusion.2 = f32[512]{0:T(512)S(1)} fusion(s32[256]{0:T(256)} %param.21, f32[256]{0:T(256)S(1)} %bitcast.374, f32[]{:T(128)} %constant.62.clone.1), kind=kCustom, calls=%fused_computation.187 | custom fusion | flops 256 | bytes 2560 | tf_op jit(solution)/shard_map/scatter-add | solution.py:168
  171.7 18.2 %all-reduce.4 = f32[512]{0:T(512)S(1)} all-reduce(f32[512]{0:T(512)S(1)} %scatter_custom_fusion.2), channel_id=6, replica_groups=mesh['tile'=8,'chan'=4] {'tile'}, use_global_device_ids=true, to_apply=%region_9.10.clone | all-reduce | flops 512 | bytes 4096
  189.9 0.6 dynamic-slice.9
  (84 shorter events, 10.7 us)
Async XLA Ops:
  6.5 12.6 %copy-start = (f32[256]{0:T(256)S(1)}, f32[256]{0:T(256)}, u32[]{:S(2)}) copy-start(f32[256]{0:T(256)} %param.19) | copy-start | bytes 3076
  6.5 22.7 %copy-start.8 = (f32[64]{0:T(128)S(1)}, f32[64]{0:T(128)}, u32[]{:S(2)}) copy-start(f32[64]{0:T(128)} %param.12) | copy-start | bytes 772
  6.5 30.5 %copy-start.5 = (bf16[16,16,256]{2,1,0:T(8,128)(2,1)S(1)}, bf16[16,16,256]{2,1,0:T(8,128)(2,1)}, u32[]{:S(2)}) copy-start(bf16[16,16,256]{2,1,0:T(8,128)(2,1)} %param.11) | copy-start | bytes 393220
  11.8 13.8 %all-to-all-start = ((s32[8,1,64]{2,1,0:T(1,128)}), s32[8,1,64]{2,1,0:T(1,128)S(1)}, u32[]{:S(2)}, u32[]{:S(2)}) async-start(s32[8,1,64]{2,1,0:T(1,128)} %all_to_all.12), calls=%async_computation | async-start | bytes 8192 | tf_op jit(solution)/shard_map/all_to_all | solution.py:117
  25.6 10.9 %all-to-all-start.1 = ((bf16[8,64,128]{2,1,0:T(8,128)(2,1)}), bf16[8,64,128]{2,1,0:T(8,128)(2,1)S(1)}, u32[]{:S(2)}, u32[]{:S(2)}) async-start(bf16[8,64,128]{2,1,0:T(8,128)(2,1)} %bitcast.24), calls=%async_computation.1 | async-start | bytes 262144 | tf_op jit(solution)/shard_map/all_to_all | solution.py:110
  29.2 54.0 %all-gather.7.cloned.1.call-start = ((), (), s32[]{:S(2)}) async-start(), calls=%async_computation.3 | async-start | bytes 1310720 | tf_op jit(solution)/shard_map/all_gather | solution.py:12
  37.2 3.7 %collective-permute-start = (bf16[4,16,256]{2,1,0:T(8,128)(2,1)S(1)}, bf16[4,16,256]{2,1,0:T(8,128)(2,1)S(1)}, u32[]{:S(2)}, u32[]{:S(2)}) collective-permute-start(bf16[4,16,256]{2,1,0:T(8,128)(2,1)S(1)} %get-tuple-element.31), channel_id=1, source_target_pairs={{0,4},{4,8},{8,12},{12,16},{16,20},{20,24},{24,28},{1,5},{5,9},{9,... | collective-permute-start | bytes 98312 | tf_op jit(solution)/shard_map/ppermute | solution.py:23
  39.3 5.8 %collective-permute-start.1 = (bf16[4,16,256]{2,1,0:T(8,128)(2,1)S(1)}, bf16[4,16,256]{2,1,0:T(8,128)(2,1)S(1)}, u32[]{:S(2)}, u32[]{:S(2)}) collective-permute-start(bf16[4,16,256]{2,1,0:T(8,128)(2,1)S(1)} %get-tuple-element.32), channel_id=1, source_target_pairs={{4,0},{8,4},{12,8},{16,12},{20,16},{24,20},{28,24},{5,1},{9,5},{13... | collective-permute-start | bytes 98312 | tf_op jit(solution)/shard_map/ppermute | solution.py:24
  53.8 0.9 copy-start.3
  57.9 5.8 %collective-permute-start.2 = (bf16[8,16,256]{2,1,0:T(8,128)(2,1)S(1)}, bf16[8,16,256]{2,1,0:T(8,128)(2,1)S(1)}, u32[]{:S(2)}, u32[]{:S(2)}) collective-permute-start(bf16[8,16,256]{2,1,0:T(8,128)(2,1)S(1)} %get-tuple-element.29), channel_id=1, source_target_pairs={{0,4},{4,8},{8,12},{12,16},{16,20},{20,24},{24,28},{1,5},{5,9},{9,... | collective-permute-start | bytes 196616 | tf_op jit(solution)/shard_map/ppermute | solution.py:23
  61.8 6.2 %collective-permute-start.3 = (bf16[8,16,256]{2,1,0:T(8,128)(2,1)S(1)}, bf16[8,16,256]{2,1,0:T(8,128)(2,1)S(1)}, u32[]{:S(2)}, u32[]{:S(2)}) collective-permute-start(bf16[8,16,256]{2,1,0:T(8,128)(2,1)S(1)} %get-tuple-element.30), channel_id=1, source_target_pairs={{4,0},{8,4},{12,8},{16,12},{20,16},{24,20},{28,24},{5,1},{9,5},{13... | collective-permute-start | bytes 196616 | tf_op jit(solution)/shard_map/ppermute | solution.py:24
  68.7 47.9 %all-gather.9.cloned.1.call-start = ((), (), s32[]{:S(2)}) async-start(), calls=%async_computation.4 | async-start | bytes 1310720 | tf_op jit(solution)/shard_map/all_gather | solution.py:12
  83.1 1.4 copy-start.2
  89.4 5.3 %collective-permute-start.4 = (bf16[8,16,256]{2,0,1:T(8,128)(2,1)S(1)}, bf16[8,16,256]{2,0,1:T(8,128)(2,1)S(1)}, u32[]{:S(2)}, u32[]{:S(2)}) collective-permute-start(bf16[8,16,256]{2,0,1:T(8,128)(2,1)S(1)} %get-tuple-element.27), channel_id=1, source_target_pairs={{0,4},{4,8},{8,12},{12,16},{16,20},{20,24},{24,28},{1,5},{5,9},{9,... | collective-permute-start | bytes 196616 | tf_op jit(solution)/shard_map/ppermute | solution.py:23
  92.8 6.2 %collective-permute-start.5 = (bf16[8,16,256]{2,0,1:T(8,128)(2,1)S(1)}, bf16[8,16,256]{2,0,1:T(8,128)(2,1)S(1)}, u32[]{:S(2)}, u32[]{:S(2)}) collective-permute-start(bf16[8,16,256]{2,0,1:T(8,128)(2,1)S(1)} %get-tuple-element.28), channel_id=1, source_target_pairs={{4,0},{8,4},{12,8},{16,12},{20,16},{24,20},{28,24},{5,1},{9,5},{13... | collective-permute-start | bytes 196616 | tf_op jit(solution)/shard_map/ppermute | solution.py:24
  116.6 1.7 copy-start.1
  122.3 5.0 %collective-permute-start.6 = (bf16[4,16,256]{2,1,0:T(8,128)(2,1)S(1)}, bf16[4,16,256]{2,1,0:T(8,128)(2,1)S(1)}, u32[]{:S(2)}, u32[]{:S(2)}) collective-permute-start(bf16[4,16,256]{2,1,0:T(8,128)(2,1)S(1)} %get-tuple-element.25), channel_id=1, source_target_pairs={{0,4},{4,8},{8,12},{12,16},{16,20},{20,24},{24,28},{1,5},{5,9},{9,... | collective-permute-start | bytes 98312 | tf_op jit(solution)/shard_map/ppermute | solution.py:23
  125.7 5.8 %collective-permute-start.7 = (bf16[4,16,256]{2,1,0:T(8,128)(2,1)S(1)}, bf16[4,16,256]{2,1,0:T(8,128)(2,1)S(1)}, u32[]{:S(2)}, u32[]{:S(2)}) collective-permute-start(bf16[4,16,256]{2,1,0:T(8,128)(2,1)S(1)} %get-tuple-element.26), channel_id=1, source_target_pairs={{4,0},{8,4},{12,8},{16,12},{20,16},{24,20},{28,24},{5,1},{9,5},{13... | collective-permute-start | bytes 98312 | tf_op jit(solution)/shard_map/ppermute | solution.py:24
  141.7 18.8 %copy-start.9 = (u32[32]{0:T(128)S(1)}, u32[32]{0:T(128)}, u32[]{:S(2)}) copy-start(u32[32]{0:T(128)} %constant.82) | copy-start | bytes 388
  142.3 26.3 %copy-start.4 = (bf16[256,128]{1,0:T(8,128)(2,1)S(1)}, bf16[256,128]{1,0:T(8,128)(2,1)}, u32[]{:S(2)}) copy-start(bf16[256,128]{1,0:T(8,128)(2,1)} %param.15) | copy-start | bytes 196612
  154.9 13.9 %copy-start.6 = (s32[256]{0:T(256)S(1)}, s32[256]{0:T(256)}, u32[]{:S(2)}) copy-start(s32[256]{0:T(256)} %param.18) | copy-start | bytes 3076
  154.9 14.2 %copy-start.7 = (s32[256]{0:T(256)S(1)}, s32[256]{0:T(256)}, u32[]{:S(2)}) copy-start(s32[256]{0:T(256)} %param.20) | copy-start | bytes 3076
  154.9 13.0 %all-to-all-start.2 = ((bf16[8,64,128]{2,1,0:T(8,128)(2,1)}), bf16[8,64,128]{2,1,0:T(8,128)(2,1)S(1)}, u32[]{:S(2)}, u32[]{:S(2)}) async-start(bf16[8,64,128]{2,1,0:T(8,128)(2,1)} %convolution_convert_fusion), calls=%async_computation.2 | async-start | bytes 262144 | tf_op jit(solution)/shard_map/all_to_all | solution.py:161
Sparse Core Ops, SparseCore 0:
  68.8 14.2 all-gather.6
  99.9 16.6 all-gather.8
